TPU v7x, 32 devices: a whole 2x2x4 slice. The times are simulated.
32 devices in a mesh: fsdp: 8 (over y, x, core), tp: 4 (over z).
Axes of the slice: x: 2, y: 2, z: 4, core: 2. Of those that a mesh axis runs over, the one named last changes fastest.
Arguments:
- block_in: bfloat16 [16, 1024, 3072], P('fsdp', 'tp'), may hold values from -6 to 6
- out_cotangent: bfloat16 [16, 1024, 3072], P('fsdp', 'tp'), may hold values from -6 to 6
- segment_ids: int32 [16, 1024], P('fsdp', 'tp'), may hold values from 0 to 3, as said below
- doc_positions: int32 [16, 1024], P('fsdp', 'tp'), may hold values from 0 to 799, as said below
- norm1_gain: bfloat16 [3072], replicated, may hold values from 0.5 to 1.5
- qkv_weight: bfloat16 [3072, 3, 3072], P('fsdp', None, 'tp'), may hold values from -0.5 to 0.5
- out_weight: bfloat16 [3072, 3072], P(('tp', 'fsdp')), may hold values from -0.875 to 0.875
- norm2_gain: bfloat16 [3072], replicated, may hold values from 0.5 to 1.5
- gate_up_weight: bfloat16 [3072, 2, 8192], P('fsdp', None, 'tp'), may hold values from -0.109375 to 0.109375
- down_weight: bfloat16 [8192, 3072], P(('tp', 'fsdp')), may hold values from -0.0625 to 0.0625
Outputs:
- block_out: bfloat16 [16, 1024, 3072], P('fsdp', 'tp')
- in_grad: float32 [16, 1024, 3072], P('fsdp', 'tp')
- norm1_gain_grad: float32 [3072], P(('fsdp', 'tp'))
- qkv_weight_grad: float32 [3072, 3, 3072], P('fsdp', None, 'tp')
- out_weight_grad: float32 [3072, 3072], P(('tp', 'fsdp'))
- norm2_gain_grad: float32 [3072], P(('fsdp', 'tp'))
- gate_up_weight_grad: float32 [3072, 2, 8192], P('fsdp', None, 'tp')
- down_weight_grad: float32 [8192, 3072], P(('tp', 'fsdp'))
Inputs may be any that keep to these rules, and one draw needn't show every extreme that they name: `segment_ids`: within each sequence the numbers start at 0, never fall and rise by at most one from a token to the next; every document has 60 to 800 tokens, and the first document of each sequence has 800. `doc_positions`: 0 at the first token of each document, else one more than at the token before.
All inputs are finite; a program needn't handle non-finite values.
Results may differ from a plain program's by a relative error of at most 0.017.
Values may be sent and summed in bfloat16 or wider, within the bound.
A program may use at most 256 MiB of HBM per device.

v0:
```python
import jax
import jax.numpy as jnp
from jax import lax
from jax.sharding import PartitionSpec as P

D = 3072
HD = 96
rms_epsilon = 1e-05
rope_theta = 10000.0
masked_score = -1e30


def rope_tables(positions, head_size):
    half_width = head_size // 2
    frequency = rope_theta ** (-(jnp.arange(half_width, dtype=jnp.float32) * 2.0 / head_size))
    angles = positions.astype(jnp.float32)[:, None] * frequency[None, :]
    return (jnp.cos(angles)[:, None, :], jnp.sin(angles)[:, None, :])


def rotate(values, cosine_part, sine_part):
    half_width = values.shape[-1] // 2
    lead_half = values[..., :half_width]
    tail_half = values[..., half_width:]
    return jnp.concatenate(
        [
            lead_half * cosine_part - tail_half * sine_part,
            tail_half * cosine_part + lead_half * sine_part,
        ],
        axis=-1,
    )


def unrotate(values, cosine_part, sine_part):
    half_width = values.shape[-1] // 2
    lead_half = values[..., :half_width]
    tail_half = values[..., half_width:]
    return jnp.concatenate(
        [
            lead_half * cosine_part + tail_half * sine_part,
            tail_half * cosine_part - lead_half * sine_part,
        ],
        axis=-1,
    )


def rms_scale(stream):
    return lax.rsqrt(jnp.mean(stream * stream, axis=-1, keepdims=True) + rms_epsilon)


def norm_back(stream, scale_rows, gain_vec, grad_rows):
    gained_grad = gain_vec * grad_rows
    input_grad = scale_rows * gained_grad - stream * scale_rows**3 * jnp.mean(
        gained_grad * stream, axis=-1, keepdims=True
    )
    return (input_grad, jnp.sum(grad_rows * stream * scale_rows, axis=0))


def allowed_mask(segment_tile, index_tile, segments):
    columns = jnp.arange(segments.shape[0], dtype=jnp.int32)
    return (segment_tile[:, None] == segments[None, :]) & (index_tile[:, None] >= columns[None, :])


def masked_scores(query_tile, key_rows, segment_tile, index_tile, segments, scale_value):
    scores = (
        jnp.einsum("qhd,khd->hqk", query_tile, key_rows, preferred_element_type=jnp.float32)
        * scale_value
    )
    return jnp.where(allowed_mask(segment_tile, index_tile, segments)[None], scores, masked_score)


def attention_forward(queries, key_rows, value_rows, segments, block_rows):
    seq_len, head_count, head_size = queries.shape
    tiles = seq_len // block_rows
    scale_value = head_size ** (-0.5)
    positions = jnp.arange(seq_len, dtype=jnp.int32)

    def query_block(packed):
        query_tile, segment_tile, index_tile = packed
        scores = masked_scores(
            query_tile, key_rows, segment_tile, index_tile, segments, scale_value
        )
        row_max = jnp.max(scores, axis=-1, keepdims=True)
        exponent = jnp.exp(scores - row_max)
        row_total = jnp.sum(exponent, axis=-1, keepdims=True)
        probs_low = (exponent / row_total).astype(jnp.bfloat16)
        mixed = jnp.einsum(
            "hqk,khd->qhd", probs_low, value_rows, preferred_element_type=jnp.float32
        )
        return (mixed, (row_max + jnp.log(row_total))[..., 0])

    mixed, log_total = lax.map(
        query_block,
        (
            queries.reshape(tiles, block_rows, head_count, head_size),
            segments.reshape(tiles, block_rows),
            positions.reshape(tiles, block_rows),
        ),
    )
    return (mixed.reshape(seq_len, head_count * head_size), log_total)


def attention_backward(queries, key_rows, value_rows, segments, log_total, out_grad, block_rows):
    seq_len, head_count, head_size = queries.shape
    tiles = seq_len // block_rows
    scale_value = head_size ** (-0.5)
    positions = jnp.arange(seq_len, dtype=jnp.int32)

    def query_block(carry, packed):
        key_acc, value_acc = carry
        query_tile, segment_tile, index_tile, total_tile, grad_tile = packed
        scores = masked_scores(
            query_tile, key_rows, segment_tile, index_tile, segments, scale_value
        )
        probs = jnp.exp(scores - total_tile[..., None])
        probs_low = probs.astype(jnp.bfloat16)
        prob_grad = jnp.einsum(
            "qhd,khd->hqk", grad_tile, value_rows, preferred_element_type=jnp.float32
        )
        score_grad = (
            probs * (prob_grad - jnp.sum(probs * prob_grad, axis=-1, keepdims=True))
        ).astype(jnp.bfloat16)
        query_grad = (
            jnp.einsum("hqk,khd->qhd", score_grad, key_rows, preferred_element_type=jnp.float32)
            * scale_value
        )
        key_acc = (
            key_acc
            + jnp.einsum("hqk,qhd->khd", score_grad, query_tile, preferred_element_type=jnp.float32)
            * scale_value
        )
        value_acc = value_acc + jnp.einsum(
            "hqk,qhd->khd", probs_low, grad_tile, preferred_element_type=jnp.float32
        )
        return ((key_acc, value_acc), query_grad)

    start_acc = (jnp.zeros(queries.shape, jnp.float32), jnp.zeros(queries.shape, jnp.float32))
    (key_grad, value_grad), query_grad = lax.scan(
        query_block,
        start_acc,
        (
            queries.reshape(tiles, block_rows, head_count, head_size),
            segments.reshape(tiles, block_rows),
            positions.reshape(tiles, block_rows),
            log_total,
            out_grad.reshape(tiles, block_rows, head_count, head_size),
        ),
    )
    return (query_grad.reshape(seq_len, head_count, head_size), key_grad, value_grad)


def gather_attention(qkv_weight, out_weight):
    return (
        lax.all_gather(qkv_weight, "fsdp", axis=0, tiled=True),
        lax.all_gather(out_weight, "fsdp", axis=0, tiled=True),
    )


def gather_feedforward(gate_up_weight, down_weight):
    return (
        lax.all_gather(gate_up_weight, "fsdp", axis=0, tiled=True),
        lax.all_gather(down_weight, "fsdp", axis=0, tiled=True),
    )


def per_device(
    block_in,
    out_cotangent,
    segment_ids,
    doc_positions,
    norm1_gain,
    qkv_weight,
    out_weight,
    norm2_gain,
    gate_up_weight,
    down_weight,
):
    micro_count = block_in.shape[0]
    fsdp_count = lax.axis_size("fsdp")
    segment_full, position_full = (
        lax.all_gather(segment_ids, "tp", axis=1, tiled=True),
        lax.all_gather(doc_positions, "tp", axis=1, tiled=True),
    )
    seq_len = segment_full.shape[1]
    block_rows = min(seq_len, 512)
    gain_one = norm1_gain.astype(jnp.float32)
    gain_two = norm2_gain.astype(jnp.float32)
    local_cols = qkv_weight.shape[2]
    local_units = gate_up_weight.shape[2]
    heads_local = local_cols // HD
    grad_qkv = jnp.zeros((D, 3, local_cols), jnp.float32)
    grad_out = jnp.zeros((out_weight.shape[0] * fsdp_count, D), jnp.float32)
    grad_gate_up = jnp.zeros((D, 2, local_units), jnp.float32)
    grad_down = jnp.zeros((down_weight.shape[0] * fsdp_count, D), jnp.float32)
    gain_one_acc = jnp.zeros((D,), jnp.float32)
    gain_two_acc = jnp.zeros((D,), jnp.float32)
    outputs = []
    input_grads = []
    for micro_index in range(micro_count):
        weights_fwd = (
            gather_attention(qkv_weight, out_weight),
            gather_feedforward(gate_up_weight, down_weight),
        )
        (qkv_full, out_full), (gate_up_full, down_full) = weights_fwd
        stream = block_in[micro_index].astype(jnp.float32)
        segment_row = segment_full[micro_index]
        cosine_part, sine_part = rope_tables(position_full[micro_index], HD)
        scale_one = rms_scale(stream)
        normed_one = (stream * scale_one * gain_one).astype(jnp.bfloat16)
        normed_one_full = lax.all_gather(normed_one, "tp", axis=0, tiled=True)
        projected = jnp.einsum(
            "sd,dtc->stc", normed_one_full, qkv_full, preferred_element_type=jnp.float32
        )
        queries = rotate(
            projected[:, 0].reshape(seq_len, heads_local, HD), cosine_part, sine_part
        ).astype(jnp.bfloat16)
        key_rows = rotate(
            projected[:, 1].reshape(seq_len, heads_local, HD), cosine_part, sine_part
        ).astype(jnp.bfloat16)
        value_rows = projected[:, 2].reshape(seq_len, heads_local, HD).astype(jnp.bfloat16)
        mixed, log_total = attention_forward(queries, key_rows, value_rows, segment_row, block_rows)
        attn_heads = mixed.astype(jnp.bfloat16)
        attn_term = jnp.dot(attn_heads, out_full, preferred_element_type=jnp.float32)
        attn_branch = lax.psum_scatter(attn_term, "tp", scatter_dimension=0, tiled=True)
        middle = stream + attn_branch
        scale_two = rms_scale(middle)
        normed_two = (middle * scale_two * gain_two).astype(jnp.bfloat16)
        normed_two_full = lax.all_gather(normed_two, "tp", axis=0, tiled=True)
        gate_up = jnp.einsum(
            "sd,dtf->stf", normed_two_full, gate_up_full, preferred_element_type=jnp.float32
        )
        gate_rows = gate_up[:, 0]
        up_rows = gate_up[:, 1]
        sigmoid_gate = jax.nn.sigmoid(gate_rows)
        silu_gate = gate_rows * sigmoid_gate
        activated = (silu_gate * up_rows).astype(jnp.bfloat16)
        mlp_term = jnp.dot(activated, down_full, preferred_element_type=jnp.float32)
        mlp_branch = lax.psum_scatter(
            mlp_term.astype(jnp.bfloat16), "tp", scatter_dimension=0, tiled=True
        ).astype(jnp.float32)
        outputs.append((middle + mlp_branch).astype(jnp.bfloat16))
        (qkv_back, out_back), (gate_up_back, down_back) = weights_fwd
        cotangent = out_cotangent[micro_index].astype(jnp.float32)
        cotangent_full = lax.all_gather(out_cotangent[micro_index], "tp", axis=0, tiled=True)
        grad_down = grad_down + jnp.einsum(
            "sf,sd->fd", activated, cotangent_full, preferred_element_type=jnp.float32
        )
        act_grad = jnp.einsum(
            "sd,fd->sf", cotangent_full, down_back, preferred_element_type=jnp.float32
        )
        gate_grad = act_grad * up_rows * sigmoid_gate * (1.0 + gate_rows * (1.0 - sigmoid_gate))
        up_grad = act_grad * silu_gate
        gate_up_grad = jnp.stack([gate_grad, up_grad], axis=1).astype(jnp.bfloat16)
        grad_gate_up = grad_gate_up + jnp.einsum(
            "sd,stf->dtf", normed_two_full, gate_up_grad, preferred_element_type=jnp.float32
        )
        normed_two_term = jnp.einsum(
            "stf,dtf->sd", gate_up_grad, gate_up_back, preferred_element_type=jnp.float32
        )
        normed_two_grad = lax.psum_scatter(normed_two_term, "tp", scatter_dimension=0, tiled=True)
        middle_back, gain_two_term = norm_back(middle, scale_two, gain_two, normed_two_grad)
        gain_two_acc = gain_two_acc + gain_two_term
        middle_grad = cotangent + middle_back
        attn_grad_full = lax.all_gather(middle_grad.astype(jnp.bfloat16), "tp", axis=0, tiled=True)
        grad_out = grad_out + jnp.einsum(
            "sc,sd->cd", attn_heads, attn_grad_full, preferred_element_type=jnp.float32
        )
        heads_grad = jnp.einsum(
            "sd,cd->sc", attn_grad_full, out_back, preferred_element_type=jnp.float32
        ).astype(jnp.bfloat16)
        query_grad, key_grad, value_grad = attention_backward(
            queries,
            key_rows,
            value_rows,
            segment_row,
            log_total,
            heads_grad.reshape(seq_len, heads_local, HD),
            block_rows,
        )
        projected_grad = jnp.stack(
            [
                unrotate(query_grad, cosine_part, sine_part).reshape(seq_len, local_cols),
                unrotate(key_grad, cosine_part, sine_part).reshape(seq_len, local_cols),
                value_grad.reshape(seq_len, local_cols),
            ],
            axis=1,
        ).astype(jnp.bfloat16)
        grad_qkv = grad_qkv + jnp.einsum(
            "sd,stc->dtc", normed_one_full, projected_grad, preferred_element_type=jnp.float32
        )
        normed_one_term = jnp.einsum(
            "stc,dtc->sd", projected_grad, qkv_back, preferred_element_type=jnp.float32
        )
        normed_one_grad = lax.psum_scatter(
            normed_one_term.astype(jnp.bfloat16), "tp", scatter_dimension=0, tiled=True
        ).astype(jnp.float32)
        stream_back, gain_one_term = norm_back(stream, scale_one, gain_one, normed_one_grad)
        gain_one_acc = gain_one_acc + gain_one_term
        input_grads.append(middle_grad + stream_back)
    owned_grads = (
        lax.psum_scatter(
            grad_qkv.astype(jnp.bfloat16), "fsdp", scatter_dimension=0, tiled=True
        ).astype(jnp.float32),
        lax.psum_scatter(
            grad_out.astype(jnp.bfloat16), "fsdp", scatter_dimension=0, tiled=True
        ).astype(jnp.float32),
        lax.psum_scatter(
            grad_gate_up.astype(jnp.bfloat16), "fsdp", scatter_dimension=0, tiled=True
        ).astype(jnp.float32),
        lax.psum_scatter(
            grad_down.astype(jnp.bfloat16), "fsdp", scatter_dimension=0, tiled=True
        ).astype(jnp.float32),
    )
    owned_gains = (
        lax.psum_scatter(gain_one_acc, ("fsdp", "tp"), scatter_dimension=0, tiled=True),
        lax.psum_scatter(gain_two_acc, ("fsdp", "tp"), scatter_dimension=0, tiled=True),
    )
    return (
        jnp.stack(outputs),
        jnp.stack(input_grads),
        owned_gains[0],
        owned_grads[0],
        owned_grads[1],
        owned_gains[1],
        owned_grads[2],
        owned_grads[3],
    )


def solution(mesh):
    in_specs = (
        P("fsdp", "tp", None),
        P("fsdp", "tp", None),
        P("fsdp", "tp"),
        P("fsdp", "tp"),
        P(),
        P("fsdp", None, "tp"),
        P(("tp", "fsdp"), None),
        P(),
        P("fsdp", None, "tp"),
        P(("tp", "fsdp"), None),
    )
    out_specs = (
        P("fsdp", "tp", None),
        P("fsdp", "tp", None),
        P(("fsdp", "tp")),
        P("fsdp", None, "tp"),
        P(("tp", "fsdp"), None),
        P(("fsdp", "tp")),
        P("fsdp", None, "tp"),
        P(("tp", "fsdp"), None),
    )
    return jax.shard_map(
        per_device, mesh=mesh, in_specs=in_specs, out_specs=out_specs, check_vma=False
    )
```

profile of v0, /device:TPU:0, one launch (start us, length us, event | category | flops | bytes accessed | tf_op | source)
XLA Modules:
  0.0 3195.4 jit_solution(16178268120911016994)
XLA Ops:
  53.0 79.6 %all-gather.15.cloned.1.call-done = bf16[1024,3072]{1,0:T(8,128)(2,1)} async-done(((bf16[256,3072]{1,0:T(8,128)(2,1)}), bf16[1024,3072]{1,0:T(8,128)(2,1)}) %all-gather.15.cloned.1.call-update) | async-done | bytes 6291472 | tf_op jit(solution)/shard_map/all_gather | solution.py:209
  132.6 82.2 %all-gather.17.cloned.1.call-done = bf16[3072,3,768]{0,2,1:T(8,128)(2,1)} async-done(((bf16[384,3,768]{0,2,1:T(8,128)(2,1)}), bf16[3072,3,768]{0,2,1:T(8,128)(2,1)}) %all-gather.17.cloned.1.call-update) | async-done | bytes 14155792 | tf_op jit(solution)/shard_map/all_gather | solution.py:153
  290.2 82.9 %all-gather.27.cloned.1.call-done = bf16[1024,3072]{1,0:T(8,128)(2,1)} async-done(((bf16[256,3072]{1,0:T(8,128)(2,1)}), bf16[1024,3072]{1,0:T(8,128)(2,1)}) %all-gather.27.cloned.1.call-update) | async-done | bytes 6291472 | tf_op jit(solution)/shard_map/all_gather | solution.py:209
  452.1 133.4 %reduce-scatter.13.cloned.1.call-done = f32[256,3072]{1,0:T(8,128)} async-done(((f32[1024,3072]{1,0:T(8,128)}), f32[256,3072]{1,0:T(8,128)}) %reduce-scatter.13.cloned.1.call-update) | async-done | bytes 3145744 | tf_op jit(solution)/shard_map/reduce_scatter | solution.py:223
  585.4 215.1 %reduce-scatter.17.cloned.1.call-done = f32[256,3072]{1,0:T(8,128)} async-done(((f32[1024,3072]{1,0:T(8,128)}), f32[256,3072]{1,0:T(8,128)}) %reduce-scatter.17.cloned.1.call-update) | async-done | bytes 3145744 | tf_op jit(solution)/shard_map/reduce_scatter | solution.py:223
  812.7 116.8 %all-gather.23.cloned.1.call-done = bf16[3072,2,2048]{2,0,1:T(8,128)(2,1)} async-done(((bf16[384,2,2048]{2,0,1:T(8,128)(2,1)}), bf16[3072,2,2048]{2,0,1:T(8,128)(2,1)}) %all-gather.23.cloned.1.call-update) | async-done | bytes 25165840 | tf_op jit(solution)/shard_map/all_gather | solution.py:160
  929.4 117.5 %all-gather.21.cloned.1.call-done = bf16[1024,3072]{1,0:T(8,128)(2,1)} async-done(((bf16[256,3072]{1,0:T(8,128)(2,1)}), bf16[1024,3072]{1,0:T(8,128)(2,1)}) %all-gather.21.cloned.1.call-update) | async-done | bytes 6291472 | tf_op jit(solution)/shard_map/all_gather | solution.py:227
  1080.4 82.4 %all-gather.35.cloned.1.call-done = bf16[1,1024,3072]{2,1,0:T(8,128)(2,1)} async-done(((bf16[1,256,3072]{2,1,0:T(8,128)(2,1)}), bf16[1,1024,3072]{2,1,0:T(8,128)(2,1)}) %all-gather.35.cloned.1.call-update) | async-done | bytes 6291472 | tf_op jit(solution)/shard_map/all_gather | solution.py:243
  1162.7 72.1 %all-gather.25.cloned.1.call-done = bf16[2048,3072]{1,0:T(8,128)(2,1)} async-done(((bf16[256,3072]{1,0:T(8,128)(2,1)}), bf16[2048,3072]{1,0:T(8,128)(2,1)}) %all-gather.25.cloned.1.call-update) | async-done | bytes 12582928 | tf_op jit(solution)/shard_map/all_gather | solution.py:161
  1260.2 34.2 %convolution_bitcast_fusion.1 = f32[1024,3072]{1,0:T(8,128)} fusion(bf16[3072,2,2048]{2,0,1:T(8,128)(2,1)} %all-gather.23.cloned.1.call-done, bf16[1024,1,2048]{2,0,1:T(8,128)(2,1)} %get-tuple-element.541, bf16[1024,1,2048]{2,0,1:T(8,128)(2,1)} %get-tuple-element.540), kind=kOutput, calls=%fused_computation.123 | convolution fusion | flops 25773998080 | bytes 46137344 | tf_op jit(solution)/shard_map/stf,dtf->sd/dot_general | solution.py:256
  1295.0 211.4 %reduce-scatter.21.cloned.1.call-done = f32[256,3072]{1,0:T(8,128)} async-done(((f32[1024,3072]{1,0:T(8,128)}), f32[256,3072]{1,0:T(8,128)}) %reduce-scatter.21.cloned.1.call-update) | async-done | bytes 3145744 | tf_op jit(solution)/shard_map/reduce_scatter | solution.py:259
  1513.2 115.7 %all-gather.29.cloned.1.call-done = bf16[1024,3072]{1,0:T(8,128)(2,1)} async-done(((bf16[256,3072]{1,0:T(8,128)(2,1)}), bf16[1024,3072]{1,0:T(8,128)(2,1)}) %all-gather.29.cloned.1.call-update) | async-done | bytes 6291472 | tf_op jit(solution)/shard_map/all_gather | solution.py:227
  1662.3 81.8 %all-gather.37.cloned.1.call-done = bf16[1,1024,3072]{2,1,0:T(8,128)(2,1)} async-done(((bf16[1,256,3072]{2,1,0:T(8,128)(2,1)}), bf16[1,1024,3072]{2,1,0:T(8,128)(2,1)}) %all-gather.37.cloned.1.call-update) | async-done | bytes 6291472 | tf_op jit(solution)/shard_map/all_gather | solution.py:243
  1840.8 172.8 %reduce-scatter.25.cloned.1.call-done = f32[256,3072]{1,0:T(8,128)} async-done(((f32[1024,3072]{1,0:T(8,128)}), f32[256,3072]{1,0:T(8,128)}) %reduce-scatter.25.cloned.1.call-update) | async-done | bytes 3145744 | tf_op jit(solution)/shard_map/reduce_scatter | solution.py:259
  2018.0 110.2 %reduce-scatter.15.cloned.1.call-done = bf16[256,3072]{1,0:T(8,128)(2,1)} async-done(((bf16[1024,3072]{1,0:T(8,128)(2,1)}), bf16[256,3072]{1,0:T(8,128)(2,1)}) %reduce-scatter.15.cloned.1.call-update) | async-done | bytes 1572880 | tf_op jit(solution)/shard_map/reduce_scatter | solution.py:237
  2128.2 114.0 %reduce-scatter.19.cloned.1.call-done = bf16[256,3072]{1,0:T(8,128)(2,1)} async-done(((bf16[1024,3072]{1,0:T(8,128)(2,1)}), bf16[256,3072]{1,0:T(8,128)(2,1)}) %reduce-scatter.19.cloned.1.call-update) | async-done | bytes 1572880 | tf_op jit(solution)/shard_map/reduce_scatter | solution.py:237
  2296.3 35.1 %fusion.71 = f32[3072,2,2048]{2,0,1:T(8,128)} fusion(bf16[1024,3072]{1,0:T(8,128)(2,1)} %all-gather.21.cloned.1.call-done, bf16[1024,1,2048]{2,0,1:T(8,128)(2,1)} %get-tuple-element.541, bf16[1024,1,2048]{2,0,1:T(8,128)(2,1)} %get-tuple-element.540), kind=kOutput, calls=%fused_computation.138 | convolution fusion | flops 25786580992 | bytes 65011712 | tf_op jit(solution)/shard_map/sd,stf->dtf/dot_general | solution.py:253
  2331.5 37.3 %add_convert_fusion = bf16[3072,2,2048]{2,0,1:T(8,128)(2,1)} fusion(f32[3072,2,2048]{2,0,1:T(8,128)} %fusion.71, bf16[1024,3072]{1,0:T(8,128)(2,1)} %all-gather.29.cloned.1.call-done, bf16[1024,1,2048]{2,0,1:T(8,128)(2,1)} %get-tuple-element.543, bf16[1024,1,2048]{2,0,1:T(8,128)(2,1)} %get-tuple-element.542), kind=kOutput, calls=%fused_computation.88 | convolution fusion | flops 25811746816 | bytes 90177536 | tf_op jit(solution)/shard_map/sd,stf->dtf/dot_general | solution.py:253
  2397.4 86.0 %all-gather.33.cloned.1.call-done = bf16[1024,3072]{1,0:T(8,128)(2,1)} async-done(((bf16[256,3072]{1,0:T(8,128)(2,1)}), bf16[1024,3072]{1,0:T(8,128)(2,1)}) %all-gather.33.cloned.1.call-update) | async-done | bytes 6291472 | tf_op jit(solution)/shard_map/all_gather | solution.py:263
  2496.8 193.2 %while.56 = (s32[]{:T(128)}, f32[1024,8,96]{0,2,1:T(8,128)S(1)}, f32[1024,8,96]{0,2,1:T(8,128)}, f32[2,512,8,96]{1,0,3,2:T(2,128)}, bf16[2,512,8,96]{1,3,2,0:T(8...) while((s32[]{:T(128)}, f32[1024,8,96]{0,2,1:T(8,128)S(1)}, ...), condition=%wide.region_20.21_spmd.clone, body=%wide.region_18.20_spmd.clone.sunk | while | flops 4070174720 | bytes 241271072 | solution.py:137
  2748.0 181.8 %while.57 = (s32[]{:T(128)}, f32[1024,8,96]{0,2,1:T(8,128)S(1)}, f32[1024,8,96]{0,2,1:T(8,128)}, f32[2,512,8,96]{1,0,3,2:T(2,128)}, bf16[2,512,8,96]{1,3,2,0:T(8...) while((s32[]{:T(128)}, f32[1024,8,96]{0,2,1:T(8,128)S(1)}, ...), condition=%wide.region_27.28_spmd.clone, body=%wide.region_25.27_spmd.clone.sunk | while | flops 4070174720 | bytes 234979584 | solution.py:137
  3032.2 46.8 %reduce-scatter.27.cloned.1.call-done = bf16[256,3072]{1,0:T(8,128)(2,1)} async-done(((bf16[1024,3072]{1,0:T(8,128)(2,1)}), bf16[256,3072]{1,0:T(8,128)(2,1)}) %reduce-scatter.27.cloned.1.call-update) | async-done | bytes 1572880 | tf_op jit(solution)/shard_map/reduce_scatter | solution.py:293
  3083.8 41.4 %all-reduce.2 = (f32[3072]{0:T(1024)S(1)}, f32[3072]{0:T(1024)S(1)}) all-reduce(f32[3072]{0:T(1024)S(1)} %add.229, f32[3072]{0:T(1024)S(1)} %add.232), channel_id=12, replica_groups=mesh['fsdp'=8,'tp'=4] {'fsdp','tp'}, use_global_device_ids=true, to_apply=%region_32.33.clone | all-reduce | flops 6144 | bytes 49152
  3134.8 50.0 %reduce-scatter.29.cloned.1.call-done = bf16[384,3,768]{2,0,1:T(8,128)(2,1)} async-done(((bf16[3072,3,768]{2,0,1:T(8,128)(2,1)}), bf16[384,3,768]{2,0,1:T(8,128)(2,1)}) %reduce-scatter.29.cloned.1.call-update) | async-done | bytes 1769488 | tf_op jit(solution)/shard_map/reduce_scatter | solution.py:300
  (419 shorter events, 1127.2 us)
Async XLA Ops:
  7.2 125.4 %all-gather.15.cloned.1.call-start = ((), (), s32[]{:S(2)}) async-start(), calls=%async_computation.12 | async-start | bytes 7864320 | tf_op jit(solution)/shard_map/all_gather | solution.py:209
  14.2 200.6 %all-gather.17.cloned.1.call-start = ((), (), s32[]{:S(2)}) async-start(), calls=%async_computation.13 | async-start | bytes 15925248 | tf_op jit(solution)/shard_map/all_gather | solution.py:153
  18.1 261.2 %all-gather.19.cloned.1.call-start = ((), (), s32[]{:S(2)}) async-start(), calls=%async_computation.14 | async-start | bytes 5308416 | tf_op jit(solution)/shard_map/all_gather | solution.py:154
  18.9 354.2 %all-gather.27.cloned.1.call-start = ((), (), s32[]{:S(2)}) async-start(), calls=%async_computation.20 | async-start | bytes 7864320 | tf_op jit(solution)/shard_map/all_gather | solution.py:209
  19.5 566.0 %reduce-scatter.13.cloned.1.call-start = ((), (), s32[]{:S(2)}) async-start(), calls=%async_computation.15 | async-start | bytes 15728640 | tf_op jit(solution)/shard_map/reduce_scatter | solution.py:223
  289.5 511.0 %reduce-scatter.17.cloned.1.call-start = ((), (), s32[]{:S(2)}) async-start(), calls=%async_computation.21 | async-start | bytes 15728640 | tf_op jit(solution)/shard_map/reduce_scatter | solution.py:223
  447.0 482.5 %all-gather.23.cloned.1.call-start = ((), (), s32[]{:S(2)}) async-start(), calls=%async_computation.17 | async-start | bytes 28311552 | tf_op jit(solution)/shard_map/all_gather | solution.py:160
  452.0 595.0 %all-gather.21.cloned.1.call-start = ((), (), s32[]{:S(2)}) async-start(), calls=%async_computation.16 | async-start | bytes 7864320 | tf_op jit(solution)/shard_map/all_gather | solution.py:227
  809.1 353.6 %all-gather.35.cloned.1.call-start = ((), (), s32[]{:S(2)}) async-start(), calls=%async_computation.34 | async-start | bytes 7864320 | tf_op jit(solution)/shard_map/all_gather | solution.py:243
  812.0 422.8 %all-gather.25.cloned.1.call-start = ((), (), s32[]{:S(2)}) async-start(), calls=%async_computation.18 | async-start | bytes 14155776 | tf_op jit(solution)/shard_map/all_gather | solution.py:161
  812.6 693.8 %reduce-scatter.21.cloned.1.call-start = ((), (), s32[]{:S(2)}) async-start(), calls=%async_computation.24 | async-start | bytes 15728640 | tf_op jit(solution)/shard_map/reduce_scatter | solution.py:259
  1294.4 334.5 %all-gather.29.cloned.1.call-start = ((), (), s32[]{:S(2)}) async-start(), calls=%async_computation.22 | async-start | bytes 7864320 | tf_op jit(solution)/shard_map/all_gather | solution.py:227
  1512.4 231.7 %all-gather.37.cloned.1.call-start = ((), (), s32[]{:S(2)}) async-start(), calls=%async_computation.35 | async-start | bytes 7864320 | tf_op jit(solution)/shard_map/all_gather | solution.py:243
  1513.1 500.5 %reduce-scatter.25.cloned.1.call-start = ((), (), s32[]{:S(2)}) async-start(), calls=%async_computation.27 | async-start | bytes 15728640 | tf_op jit(solution)/shard_map/reduce_scatter | solution.py:259
  1803.4 324.8 %reduce-scatter.15.cloned.1.call-start = ((), (), s32[]{:S(2)}) async-start(), calls=%async_computation.19 | async-start | bytes 7864320 | tf_op jit(solution)/shard_map/reduce_scatter | solution.py:237
  1821.8 420.4 %reduce-scatter.19.cloned.1.call-start = ((), (), s32[]{:S(2)}) async-start(), calls=%async_computation.23 | async-start | bytes 7864320 | tf_op jit(solution)/shard_map/reduce_scatter | solution.py:237
  1840.2 528.9 %all-gather.31.cloned.1.call-start = ((), (), s32[]{:S(2)}) async-start(), calls=%async_computation.25 | async-start | bytes 7864320 | tf_op jit(solution)/shard_map/all_gather | solution.py:263
  2252.3 231.1 %all-gather.33.cloned.1.call-start = ((), (), s32[]{:S(2)}) async-start(), calls=%async_computation.28 | async-start | bytes 7864320 | tf_op jit(solution)/shard_map/all_gather | solution.py:263
  2252.9 763.4 %reduce-scatter.35.cloned.1.call-start = ((), (), s32[]{:S(2)}) async-start(), calls=%async_computation.33 | async-start | bytes 14155776 | tf_op jit(solution)/shard_map/reduce_scatter | solution.py:309
  2296.1 725.8 %reduce-scatter.33.cloned.1.call-start = ((), (), s32[]{:S(2)}) async-start(), calls=%async_computation.32 | async-start | bytes 28311552 | tf_op jit(solution)/shard_map/reduce_scatter | solution.py:306
  2368.8 661.2 %reduce-scatter.31.cloned.1.call-start = ((), (), s32[]{:S(2)}) async-start(), calls=%async_computation.31 | async-start | bytes 5308416 | tf_op jit(solution)/shard_map/reduce_scatter | solution.py:303
  2493.8 538.4 %reduce-scatter.23.cloned.1.call-start = ((), (), s32[]{:S(2)}) async-start(), calls=%async_computation.26 | async-start | bytes 7864320 | tf_op jit(solution)/shard_map/reduce_scatter | solution.py:293
  2745.3 333.8 %reduce-scatter.27.cloned.1.call-start = ((), (), s32[]{:S(2)}) async-start(), calls=%async_computation.29 | async-start | bytes 7864320 | tf_op jit(solution)/shard_map/reduce_scatter | solution.py:293
  2968.7 216.1 %reduce-scatter.29.cloned.1.call-start = ((), (), s32[]{:S(2)}) async-start(), calls=%async_computation.30 | async-start | bytes 15925248 | tf_op jit(solution)/shard_map/reduce_scatter | solution.py:300
  (94 other events, 5655.4 us)
Sparse Core Ops, SparseCore 0:
  14.3 118.2 all-gather.14
  135.0 79.7 all-gather.16
  216.7 38.9 all-gather.18
  257.7 115.4 all-gather.26
  375.3 210.0 reduce-scatter.12
  587.6 212.8 reduce-scatter.16
  803.0 126.3 all-gather.22
  931.6 115.3 all-gather.20
  1049.1 113.5 all-gather.34
  1164.5 70.3 all-gather.24
  1294.5 211.8 reduce-scatter.20
  1512.5 116.3 all-gather.28
  1630.5 113.5 all-gather.36
  1803.5 210.0 reduce-scatter.24
  2016.3 111.7 reduce-scatter.14
  2130.9 111.2 reduce-scatter.18
  2252.5 115.8 all-gather.30
  2369.8 113.5 all-gather.32
  2486.9 90.6 reduce-scatter.34
  2581.0 156.8 reduce-scatter.32
  2741.4 53.8 reduce-scatter.30
  2798.3 110.7 reduce-scatter.22
  2968.8 110.1 reduce-scatter.26
  3082.9 101.8 reduce-scatter.28
where the time goes:
time: 3210 us; the launch traced here: 3200 us
  waiting for transfers between devices  1970 us (61%)
  matrix products  733 us (23%)
  local copies, waits for them, and re-layouts  233 us (7%)
  other arithmetic  165 us (5%)
  blocking collectives  71.3 us (2%)
    reduce_scatter x2, waiting for transfers between devices, per_device(): lax.psum_scatter(normed_two_term, 'tp', scatter_dimension=0, tiled=True)  384 us
    reduce_scatter x2, waiting for transfers between devices, per_device(): lax.psum_scatter(attn_term, 'tp', scatter_dimension=0, tiled=True)  348 us
    all_gather x2, waiting for transfers between devices, per_device(): normed_two_full = lax.all_gather(normed_two, 'tp', axis=0, tiled=True)  233 us
    reduce_scatter x2, waiting for transfers between devices, per_device(): lax.psum_scatter(mlp_term.astype(jnp.bfloat16), 'tp', scatter_dimension=0...  224 us
    all_gather x2, waiting for transfers between devices, per_device(): lax.all_gather(out_cotangent[micro_index], 'tp', axis=0, tiled=True)  164 us
    all_gather x2, waiting for transfers between devices, per_device(): normed_one_full = lax.all_gather(normed_one, 'tp', axis=0, tiled=True)  163 us
    dynamic_update_slice x8, local copies, waits for them, and re-layouts, attention_forward(): lax.map(query_block, (queries.reshape(tiles, block_rows, head_count, head...  127 us
    all_gather x1, waiting for transfers between devices, gather_feedforward(): lax.all_gather(gate_up_weight, 'fsdp', axis=0, tiled=True)  117 us
  transfers between devices with their start and end apart: 24, of which 18 were waited for; matrix products, arithmetic and copies ran while one was open for 30% of the time, Pallas kernels for 0%

commit v1 on v0

--- a/solution.py
+++ b/solution.py
@@ -1,3 +1,4 @@
+import functools
 import jax
 import jax.numpy as jnp
 from jax import lax
@@ -8,6 +9,26 @@
 rms_epsilon = 1e-05
 rope_theta = 10000.0
 masked_score = -1e30
+
+
+def reach_columns(target, mesh_dim):
+    local_out, moved, back = (lax.axis_size(mesh_dim), lax.axis_index(mesh_dim), target.shape[0])
+    v1, view_out = (target, 1)
+    while view_out < local_out:
+        v1 = jnp.concatenate(
+            [
+                v1,
+                lax.ppermute(
+                    v1, mesh_dim, [(q, (q - view_out) % local_out) for q in range(local_out)]
+                ),
+            ],
+            axis=0,
+        )
+        view_out = 2 * view_out
+    return jnp.roll(v1, moved * back, axis=0)
+
+
+list_files = functools.partial(reach_columns, mesh_dim="tp")
 
 
 def rope_tables(positions, head_size):
@@ -260,7 +281,7 @@
         middle_back, gain_two_term = norm_back(middle, scale_two, gain_two, normed_two_grad)
         gain_two_acc = gain_two_acc + gain_two_term
         middle_grad = cotangent + middle_back
-        attn_grad_full = lax.all_gather(middle_grad.astype(jnp.bfloat16), "tp", axis=0, tiled=True)
+        attn_grad_full = list_files(middle_grad.astype(jnp.bfloat16))
         grad_out = grad_out + jnp.einsum(
             "sc,sd->cd", attn_heads, attn_grad_full, preferred_element_type=jnp.float32
         )

time: 3210 us -> 3420 us (1.065)
  waiting for transfers between devices: 1970 us -> 2140 us
  other arithmetic: 165 us -> 205 us
    ppermute x0 -> x4, waiting for transfers between devices: none -> 292 us  [reach_columns(): lax.ppermute(v1, mesh_dim, [(q, (q - view_out) % local_out) for q in rang...]
    all_gather x2 -> x0, waiting for transfers between devices: 86 us -> none  [per_device(): lax.all_gather(middle_grad.astype(jnp.bfloat16), 'tp', axis=0, tiled=True)]
    reduce_scatter x2, waiting for transfers between devices: 384 us -> 341 us  [per_device(): lax.psum_scatter(normed_two_term, 'tp', scatter_dimension=0, tiled=True)]
    concatenate x0 -> x4, other arithmetic: none -> 40.2 us  [the longest x2 36.9 us: reach_columns(): return jnp.roll(v1, moved * back, axis=0)]
  transfers between devices with their start and end apart: 24 -> 26, of which waited for: 18 -> 20; matrix products, arithmetic and copies ran while one was open for 30% -> 29% of each run, Pallas kernels for 0% -> 0%
where the time goes in v1:
time: 3420 us; the launch traced here: 3410 us
  waiting for transfers between devices  2140 us (63%)
  matrix products  726 us (21%)
  local copies, waits for them, and re-layouts  234 us (7%)
  other arithmetic  205 us (6%)
  blocking collectives  71.3 us (2%)
    reduce_scatter x2, waiting for transfers between devices, per_device(): lax.psum_scatter(attn_term, 'tp', scatter_dimension=0, tiled=True)  349 us
    reduce_scatter x2, waiting for transfers between devices, per_device(): lax.psum_scatter(normed_two_term, 'tp', scatter_dimension=0, tiled=True)  341 us
    ppermute x4, waiting for transfers between devices, reach_columns(): lax.ppermute(v1, mesh_dim, [(q, (q - view_out) % local_out) for q in rang...  292 us
    all_gather x2, waiting for transfers between devices, per_device(): normed_two_full = lax.all_gather(normed_two, 'tp', axis=0, tiled=True)  233 us
    reduce_scatter x2, waiting for transfers between devices, per_device(): lax.psum_scatter(mlp_term.astype(jnp.bfloat16), 'tp', scatter_dimension=0...  224 us
    all_gather x2, waiting for transfers between devices, per_device(): lax.all_gather(out_cotangent[micro_index], 'tp', axis=0, tiled=True)  164 us
    all_gather x2, waiting for transfers between devices, per_device(): normed_one_full = lax.all_gather(normed_one, 'tp', axis=0, tiled=True)  162 us
    dynamic_update_slice x8, local copies, waits for them, and re-layouts, attention_forward(): lax.map(query_block, (queries.reshape(tiles, block_rows, head_count, head...  127 us
  transfers between devices with their start and end apart: 26, of which 20 were waited for; matrix products, arithmetic and copies ran while one was open for 29% of the time, Pallas kernels for 0%

profile of v1, /device:TPU:0, one launch (start us, length us, event | category | flops | bytes accessed | tf_op | source)
XLA Modules:
  0.0 3405.0 jit_solution(17081230155773689960)
XLA Ops:
  52.9 79.6 %all-gather.13.cloned.1.call-done = bf16[1024,3072]{1,0:T(8,128)(2,1)} async-done(((bf16[256,3072]{1,0:T(8,128)(2,1)}), bf16[1024,3072]{1,0:T(8,128)(2,1)}) %all-gather.13.cloned.1.call-update) | async-done | bytes 6291472 | tf_op jit(solution)/shard_map/all_gather | solution.py:230
  132.5 82.2 %all-gather.15.cloned.1.call-done = bf16[3072,3,768]{0,2,1:T(8,128)(2,1)} async-done(((bf16[384,3,768]{0,2,1:T(8,128)(2,1)}), bf16[3072,3,768]{0,2,1:T(8,128)(2,1)}) %all-gather.15.cloned.1.call-update) | async-done | bytes 14155792 | tf_op jit(solution)/shard_map/all_gather | solution.py:174
  239.6 34.1 %while.54 = (s32[]{:T(128)}, bf16[2,512,8,96]{1,3,2,0:T(8,128)(2,1)}, f32[2,8,512]{2,1,0:T(8,128)S(1)}, s32[2,512]{1,0:T(2,128)S(1)}, s32[1,1024]{1,0:T(1,128)S(...) while((s32[]{:T(128)}, ...), condition=%wide.region_4.5_spmd, body=%wide.region_1.4_spmd.sunk | while | flops 1662513152 | bytes 70664376 | solution.py:112
  290.4 82.6 %all-gather.25.cloned.1.call-done = bf16[1024,3072]{1,0:T(8,128)(2,1)} async-done(((bf16[256,3072]{1,0:T(8,128)(2,1)}), bf16[1024,3072]{1,0:T(8,128)(2,1)}) %all-gather.25.cloned.1.call-update) | async-done | bytes 6291472 | tf_op jit(solution)/shard_map/all_gather | solution.py:230
  451.6 133.8 %reduce-scatter.13.cloned.1.call-done = f32[256,3072]{1,0:T(8,128)} async-done(((f32[1024,3072]{1,0:T(8,128)}), f32[256,3072]{1,0:T(8,128)}) %reduce-scatter.13.cloned.1.call-update) | async-done | bytes 3145744 | tf_op jit(solution)/shard_map/reduce_scatter | solution.py:244
  585.3 215.1 %reduce-scatter.17.cloned.1.call-done = f32[256,3072]{1,0:T(8,128)} async-done(((f32[1024,3072]{1,0:T(8,128)}), f32[256,3072]{1,0:T(8,128)}) %reduce-scatter.17.cloned.1.call-update) | async-done | bytes 3145744 | tf_op jit(solution)/shard_map/reduce_scatter | solution.py:244
  812.6 116.8 %all-gather.21.cloned.1.call-done = bf16[3072,2,2048]{2,0,1:T(8,128)(2,1)} async-done(((bf16[384,2,2048]{2,0,1:T(8,128)(2,1)}), bf16[3072,2,2048]{2,0,1:T(8,128)(2,1)}) %all-gather.21.cloned.1.call-update) | async-done | bytes 25165840 | tf_op jit(solution)/shard_map/all_gather | solution.py:181
  929.4 117.5 %all-gather.19.cloned.1.call-done = bf16[1024,3072]{1,0:T(8,128)(2,1)} async-done(((bf16[256,3072]{1,0:T(8,128)(2,1)}), bf16[1024,3072]{1,0:T(8,128)(2,1)}) %all-gather.19.cloned.1.call-update) | async-done | bytes 6291472 | tf_op jit(solution)/shard_map/all_gather | solution.py:248
  1080.2 82.5 %all-gather.29.cloned.1.call-done = bf16[1,1024,3072]{2,1,0:T(8,128)(2,1)} async-done(((bf16[1,256,3072]{2,1,0:T(8,128)(2,1)}), bf16[1,1024,3072]{2,1,0:T(8,128)(2,1)}) %all-gather.29.cloned.1.call-update) | async-done | bytes 6291472 | tf_op jit(solution)/shard_map/all_gather | solution.py:264
  1162.7 72.1 %all-gather.23.cloned.1.call-done = bf16[2048,3072]{1,0:T(8,128)(2,1)} async-done(((bf16[256,3072]{1,0:T(8,128)(2,1)}), bf16[2048,3072]{1,0:T(8,128)(2,1)}) %all-gather.23.cloned.1.call-update) | async-done | bytes 12582928 | tf_op jit(solution)/shard_map/all_gather | solution.py:182
  1294.6 211.4 %reduce-scatter.21.cloned.1.call-done = f32[256,3072]{1,0:T(8,128)} async-done(((f32[1024,3072]{1,0:T(8,128)}), f32[256,3072]{1,0:T(8,128)}) %reduce-scatter.21.cloned.1.call-update) | async-done | bytes 3145744 | tf_op jit(solution)/shard_map/reduce_scatter | solution.py:280
  1512.8 115.8 %all-gather.27.cloned.1.call-done = bf16[1024,3072]{1,0:T(8,128)(2,1)} async-done(((bf16[256,3072]{1,0:T(8,128)(2,1)}), bf16[1024,3072]{1,0:T(8,128)(2,1)}) %all-gather.27.cloned.1.call-update) | async-done | bytes 6291472 | tf_op jit(solution)/shard_map/all_gather | solution.py:248
  1661.8 81.9 %all-gather.31.cloned.1.call-done = bf16[1,1024,3072]{2,1,0:T(8,128)(2,1)} async-done(((bf16[1,256,3072]{2,1,0:T(8,128)(2,1)}), bf16[1,1024,3072]{2,1,0:T(8,128)(2,1)}) %all-gather.31.cloned.1.call-update) | async-done | bytes 6291472 | tf_op jit(solution)/shard_map/all_gather | solution.py:264
  1883.8 129.5 %reduce-scatter.25.cloned.1.call-done = f32[256,3072]{1,0:T(8,128)} async-done(((f32[1024,3072]{1,0:T(8,128)}), f32[256,3072]{1,0:T(8,128)}) %reduce-scatter.25.cloned.1.call-update) | async-done | bytes 3145744 | tf_op jit(solution)/shard_map/reduce_scatter | solution.py:280
  2017.7 110.2 %reduce-scatter.15.cloned.1.call-done = bf16[256,3072]{1,0:T(8,128)(2,1)} async-done(((bf16[1024,3072]{1,0:T(8,128)(2,1)}), bf16[256,3072]{1,0:T(8,128)(2,1)}) %reduce-scatter.15.cloned.1.call-update) | async-done | bytes 1572880 | tf_op jit(solution)/shard_map/reduce_scatter | solution.py:258
  2127.9 114.0 %reduce-scatter.19.cloned.1.call-done = bf16[256,3072]{1,0:T(8,128)(2,1)} async-done(((bf16[1024,3072]{1,0:T(8,128)(2,1)}), bf16[256,3072]{1,0:T(8,128)(2,1)}) %reduce-scatter.19.cloned.1.call-update) | async-done | bytes 1572880 | tf_op jit(solution)/shard_map/reduce_scatter | solution.py:258
  2328.3 35.2 %fusion.81 = f32[3072,2,2048]{2,0,1:T(8,128)} fusion(bf16[1024,3072]{1,0:T(8,128)(2,1)} %all-gather.19.cloned.1.call-done, bf16[1024,1,2048]{2,0,1:T(8,128)(2,1)} %get-tuple-element.542, bf16[1024,1,2048]{2,0,1:T(8,128)(2,1)} %get-tuple-element.541), kind=kOutput, calls=%fused_computation.160 | convolution fusion | flops 25786580992 | bytes 65011712 | tf_op jit(solution)/shard_map/sd,stf->dtf/dot_general | solution.py:274
  2363.5 229.8 %collective-permute-done.3 = bf16[512,3072]{1,0:T(8,128)(2,1)S(1)} collective-permute-done((bf16[512,3072]{1,0:T(8,128)(2,1)S(1)}, bf16[512,3072]{1,0:T(8,128)(2,1)S(1)}, u32[]{:S(2)}, u32[]{:S(2)}) %collective-permute-start.3) | collective-permute-done | bytes 3145760 | tf_op jit(solution)/shard_map/ppermute | solution.py:21
  2647.3 38.3 %add_convert_fusion = bf16[3072,2,2048]{2,0,1:T(8,128)(2,1)} fusion(f32[3072,2,2048]{2,0,1:T(8,128)} %fusion.81, bf16[1024,3072]{1,0:T(8,128)(2,1)} %all-gather.27.cloned.1.call-done, bf16[1024,1,2048]{2,0,1:T(8,128)(2,1)} %get-tuple-element.544, bf16[1024,1,2048]{2,0,1:T(8,128)(2,1)} %get-tuple-element.543), kind=kOutput, calls=%fused_computation.88 | convolution fusion | flops 25811746816 | bytes 90177536 | tf_op jit(solution)/shard_map/sd,stf->dtf/dot_general | solution.py:274
  2706.9 192.7 %while.56 = (s32[]{:T(128)}, f32[1024,8,96]{0,2,1:T(8,128)S(1)}, f32[1024,8,96]{0,2,1:T(8,128)}, f32[2,512,8,96]{1,0,3,2:T(2,128)}, bf16[2,512,8,96]{1,3,2,0:T(8...) while((s32[]{:T(128)}, f32[1024,8,96]{0,2,1:T(8,128)S(1)}, ...), condition=%wide.region_20.22_spmd.clone, body=%wide.region_18.21_spmd.clone.sunk | while | flops 4070174720 | bytes 241271072 | solution.py:158
  2957.4 180.5 %while.57 = (s32[]{:T(128)}, f32[1024,8,96]{0,2,1:T(8,128)S(1)}, f32[1024,8,96]{0,2,1:T(8,128)}, f32[2,512,8,96]{1,0,3,2:T(2,128)}, bf16[2,512,8,96]{1,3,2,0:T(8...) while((s32[]{:T(128)}, f32[1024,8,96]{0,2,1:T(8,128)S(1)}, ...), condition=%wide.region_27.29_spmd.clone, body=%wide.region_25.28_spmd.clone.sunk | while | flops 4070174720 | bytes 234979584 | solution.py:158
  3240.2 48.2 %reduce-scatter.27.cloned.1.call-done = bf16[256,3072]{1,0:T(8,128)(2,1)} async-done(((bf16[1024,3072]{1,0:T(8,128)(2,1)}), bf16[256,3072]{1,0:T(8,128)(2,1)}) %reduce-scatter.27.cloned.1.call-update) | async-done | bytes 1572880 | tf_op jit(solution)/shard_map/reduce_scatter | solution.py:314
  3293.2 41.4 %all-reduce.2 = (f32[3072]{0:T(1024)S(1)}, f32[3072]{0:T(1024)S(1)}) all-reduce(f32[3072]{0:T(1024)S(1)} %add.237, f32[3072]{0:T(1024)S(1)} %add.240), channel_id=12, replica_groups=mesh['fsdp'=8,'tp'=4] {'fsdp','tp'}, use_global_device_ids=true, to_apply=%region_32.34.clone | all-reduce | flops 6144 | bytes 49152
  3344.2 50.2 %reduce-scatter.29.cloned.1.call-done = bf16[384,3,768]{2,0,1:T(8,128)(2,1)} async-done(((bf16[3072,3,768]{2,0,1:T(8,128)(2,1)}), bf16[384,3,768]{2,0,1:T(8,128)(2,1)}) %reduce-scatter.29.cloned.1.call-update) | async-done | bytes 1769488 | tf_op jit(solution)/shard_map/reduce_scatter | solution.py:321
  (435 shorter events, 1233.1 us)
Async XLA Ops:
  7.2 125.4 %all-gather.13.cloned.1.call-start = ((), (), s32[]{:S(2)}) async-start(), calls=%async_computation.12 | async-start | bytes 7864320 | tf_op jit(solution)/shard_map/all_gather | solution.py:230
  14.2 200.6 %all-gather.15.cloned.1.call-start = ((), (), s32[]{:S(2)}) async-start(), calls=%async_computation.13 | async-start | bytes 15925248 | tf_op jit(solution)/shard_map/all_gather | solution.py:174
  18.1 261.5 %all-gather.17.cloned.1.call-start = ((), (), s32[]{:S(2)}) async-start(), calls=%async_computation.14 | async-start | bytes 5308416 | tf_op jit(solution)/shard_map/all_gather | solution.py:175
  18.8 354.2 %all-gather.25.cloned.1.call-start = ((), (), s32[]{:S(2)}) async-start(), calls=%async_computation.20 | async-start | bytes 7864320 | tf_op jit(solution)/shard_map/all_gather | solution.py:230
  19.4 565.9 %reduce-scatter.13.cloned.1.call-start = ((), (), s32[]{:S(2)}) async-start(), calls=%async_computation.15 | async-start | bytes 15728640 | tf_op jit(solution)/shard_map/reduce_scatter | solution.py:244
  289.7 510.8 %reduce-scatter.17.cloned.1.call-start = ((), (), s32[]{:S(2)}) async-start(), calls=%async_computation.21 | async-start | bytes 15728640 | tf_op jit(solution)/shard_map/reduce_scatter | solution.py:244
  446.5 482.9 %all-gather.21.cloned.1.call-start = ((), (), s32[]{:S(2)}) async-start(), calls=%async_computation.17 | async-start | bytes 28311552 | tf_op jit(solution)/shard_map/all_gather | solution.py:181
  451.5 595.4 %all-gather.19.cloned.1.call-start = ((), (), s32[]{:S(2)}) async-start(), calls=%async_computation.16 | async-start | bytes 7864320 | tf_op jit(solution)/shard_map/all_gather | solution.py:248
  809.1 353.6 %all-gather.29.cloned.1.call-start = ((), (), s32[]{:S(2)}) async-start(), calls=%async_computation.32 | async-start | bytes 7864320 | tf_op jit(solution)/shard_map/all_gather | solution.py:264
  811.9 422.9 %all-gather.23.cloned.1.call-start = ((), (), s32[]{:S(2)}) async-start(), calls=%async_computation.18 | async-start | bytes 14155776 | tf_op jit(solution)/shard_map/all_gather | solution.py:182
  812.5 693.4 %reduce-scatter.21.cloned.1.call-start = ((), (), s32[]{:S(2)}) async-start(), calls=%async_computation.24 | async-start | bytes 15728640 | tf_op jit(solution)/shard_map/reduce_scatter | solution.py:280
  1294.0 334.6 %all-gather.27.cloned.1.call-start = ((), (), s32[]{:S(2)}) async-start(), calls=%async_computation.22 | async-start | bytes 7864320 | tf_op jit(solution)/shard_map/all_gather | solution.py:248
  1512.0 231.7 %all-gather.31.cloned.1.call-start = ((), (), s32[]{:S(2)}) async-start(), calls=%async_computation.33 | async-start | bytes 7864320 | tf_op jit(solution)/shard_map/all_gather | solution.py:264
  1512.7 500.6 %reduce-scatter.25.cloned.1.call-start = ((), (), s32[]{:S(2)}) async-start(), calls=%async_computation.26 | async-start | bytes 15728640 | tf_op jit(solution)/shard_map/reduce_scatter | solution.py:280
  1803.1 324.8 %reduce-scatter.15.cloned.1.call-start = ((), (), s32[]{:S(2)}) async-start(), calls=%async_computation.19 | async-start | bytes 7864320 | tf_op jit(solution)/shard_map/reduce_scatter | solution.py:258
  1821.5 420.4 %reduce-scatter.19.cloned.1.call-start = ((), (), s32[]{:S(2)}) async-start(), calls=%async_computation.23 | async-start | bytes 7864320 | tf_op jit(solution)/shard_map/reduce_scatter | solution.py:258
  1839.9 1384.5 %reduce-scatter.35.cloned.1.call-start = ((), (), s32[]{:S(2)}) async-start(), calls=%async_computation.31 | async-start | bytes 14155776 | tf_op jit(solution)/shard_map/reduce_scatter | solution.py:330
  1883.2 1346.7 %reduce-scatter.31.cloned.1.call-start = ((), (), s32[]{:S(2)}) async-start(), calls=%async_computation.29 | async-start | bytes 5308416 | tf_op jit(solution)/shard_map/reduce_scatter | solution.py:324
  2291.6 327.6 %collective-permute-start.1 = (bf16[512,3072]{1,0:T(8,128)(2,1)S(1)}, bf16[512,3072]{1,0:T(8,128)(2,1)S(1)}, u32[]{:S(2)}, u32[]{:S(2)}) collective-permute-start(bf16[512,3072]{1,0:T(8,128)(2,1)S(1)} %pad_maximum_fusion.10), channel_id=1, source_target_pairs={{0,2},{1,3},{2,0},{3,1},{4,6},{5,7},{6,4},{7,5},{8,10},{9,11},{10,... | collective-permute-start | bytes 9437192 | tf_op jit(solution)/shard_map/ppermute | solution.py:21
  2325.1 268.2 %collective-permute-start.3 = (bf16[512,3072]{1,0:T(8,128)(2,1)S(1)}, bf16[512,3072]{1,0:T(8,128)(2,1)S(1)}, u32[]{:S(2)}, u32[]{:S(2)}) collective-permute-start(bf16[512,3072]{1,0:T(8,128)(2,1)S(1)} %pad_maximum_fusion.11), channel_id=1, source_target_pairs={{0,2},{1,3},{2,0},{3,1},{4,6},{5,7},{6,4},{7,5},{8,10},{9,11},{10,... | collective-permute-start | bytes 9437192 | tf_op jit(solution)/shard_map/ppermute | solution.py:21
  2647.2 584.9 %reduce-scatter.33.cloned.1.call-start = ((), (), s32[]{:S(2)}) async-start(), calls=%async_computation.30 | async-start | bytes 28311552 | tf_op jit(solution)/shard_map/reduce_scatter | solution.py:327
  2685.6 554.6 %reduce-scatter.23.cloned.1.call-start = ((), (), s32[]{:S(2)}) async-start(), calls=%async_computation.25 | async-start | bytes 7864320 | tf_op jit(solution)/shard_map/reduce_scatter | solution.py:314
  2954.7 333.8 %reduce-scatter.27.cloned.1.call-start = ((), (), s32[]{:S(2)}) async-start(), calls=%async_computation.27 | async-start | bytes 7864320 | tf_op jit(solution)/shard_map/reduce_scatter | solution.py:314
  3176.7 217.6 %reduce-scatter.29.cloned.1.call-start = ((), (), s32[]{:S(2)}) async-start(), calls=%async_computation.28 | async-start | bytes 15925248 | tf_op jit(solution)/shard_map/reduce_scatter | solution.py:321
  (101 other events, 5810.9 us)
Sparse Core Ops, SparseCore 0:
  14.3 118.2 all-gather.12
  135.0 79.7 all-gather.14
  216.7 38.9 all-gather.16
  257.6 115.3 all-gather.24
  375.2 210.0 reduce-scatter.12
  587.5 212.8 reduce-scatter.16
  802.9 126.3 all-gather.20
  931.5 115.3 all-gather.18
  1049.0 113.5 all-gather.28
  1164.4 70.3 all-gather.22
  1294.1 211.8 reduce-scatter.20
  1512.1 116.3 all-gather.26
  1630.1 113.5 all-gather.30
  1803.2 210.0 reduce-scatter.24
  2016.0 111.7 reduce-scatter.14
  2130.6 111.2 reduce-scatter.18
  2245.3 92.9 reduce-scatter.34
  2647.3 54.5 reduce-scatter.30
  2706.0 156.8 reduce-scatter.32
  2954.8 111.3 reduce-scatter.22
  3176.9 111.5 reduce-scatter.26
  3292.5 101.8 reduce-scatter.28
